TPU v7x, 32 devices: a whole 2x2x4 slice. The times are simulated.
32 devices in a mesh: shard: 2 (over x), ctx: 4 (over y, core), tp: 4 (over z).
Axes of the slice: x: 2, y: 2, z: 4, core: 2. Of those that a mesh axis runs over, the one named last changes fastest.
Arguments:
- tokens: bfloat16 [4, 4096, 1024], P('shard', ('ctx', 'tp')), may hold values from -6 to 6
- positions: int32 [4, 4096], P('shard', 'ctx'), may hold values from 0 to 12287, as said below
- first_gain: float32 [1024], replicated, may hold values from 0.5 to 1.5
- query_weight: bfloat16 [1024, 1024], P(('shard', 'ctx'), 'tp'), may hold values from -0.1875 to 0.1875
- key_weight: bfloat16 [1024, 512], P(('shard', 'ctx'), 'tp'), may hold values from -0.1875 to 0.1875
- value_weight: bfloat16 [1024, 512], P(('shard', 'ctx'), 'tp'), may hold values from -0.1875 to 0.1875
- query_gain: float32 [64], replicated, may hold values from 0.1 to 1.9
- key_gain: float32 [64], replicated, may hold values from 0.1 to 1.9
- output_weight: bfloat16 [1024, 1024], P('tp', ('shard', 'ctx')), may hold values from -1 to 1
- second_gain: float32 [1024], replicated, may hold values from 0.5 to 1.5
- gate_weight: bfloat16 [1024, 4608], P(('shard', 'ctx'), 'tp'), may hold values from -0.1875 to 0.1875
- up_weight: bfloat16 [1024, 4608], P(('shard', 'ctx'), 'tp'), may hold values from -0.1875 to 0.1875
- down_weight: bfloat16 [4608, 1024], P('tp', ('shard', 'ctx')), may hold values from -0.09375 to 0.09375
- upstream: bfloat16 [4, 4096, 1024], P('shard', ('ctx', 'tp')), may hold values from -6 to 6
Outputs:
- block_output: bfloat16 [4, 4096, 1024], P('shard', ('ctx', 'tp'))
- token_gradient: float32 [4, 4096, 1024], P('shard', ('ctx', 'tp'))
- query_gradient: float32 [1024, 1024], P(('shard', 'ctx'), 'tp')
- key_gradient: float32 [1024, 512], P(('shard', 'ctx'), 'tp')
- value_gradient: float32 [1024, 512], P(('shard', 'ctx'), 'tp')
- output_gradient: float32 [1024, 1024], P('tp', ('shard', 'ctx'))
- gate_gradient: float32 [1024, 4608], P(('shard', 'ctx'), 'tp')
- up_gradient: float32 [1024, 4608], P(('shard', 'ctx'), 'tp')
- down_gradient: float32 [4608, 1024], P('tp', ('shard', 'ctx'))
- first_gain_gradient: float32 [1024], replicated
- second_gain_gradient: float32 [1024], replicated
- query_gain_gradient: float32 [64], replicated
- key_gain_gradient: float32 [64], replicated
Inputs may be any that keep to these rules, and one draw needn't show every extreme that they name: `positions`: along each sequence a position exceeds the one before it by 1 to 3; the first is at most 2.
All inputs are finite; a program needn't handle non-finite values.
Results may differ from a plain program's by a relative error of at most 0.02.
Values may be sent and summed in bfloat16 or wider, within the bound.
No kernel may reach another device: no remote copies, remote signals or barrier semaphores. Data moves between devices by JAX's collectives and lax.ppermute only.
A program may use at most 192 MiB of HBM per device.

v0:
```python
import math
import jax
import jax.numpy as jnp
from jax import lax
from jax.sharding import PartitionSpec as P

EPS = 1e-05
THETA = 1000000.0
NEGATIVE = -1e30


def norm_rows(values, gain):
    return values * lax.rsqrt(jnp.mean(values * values, axis=-1, keepdims=True) + EPS) * gain


def rotary_tables(places, width):
    freqs = jnp.exp(-math.log(THETA) * jnp.arange(0, width, 2).astype(jnp.float32) / width)
    angles = places.astype(jnp.float32)[:, None] * freqs[None, :]
    cosine = jnp.concatenate([jnp.cos(angles), jnp.cos(angles)], axis=-1)[:, None, :]
    sine = jnp.concatenate([jnp.sin(angles), jnp.sin(angles)], axis=-1)[:, None, :]
    return (cosine, sine)


def shape_heads(raw, gain, cosine, sine):
    normed = norm_rows(raw, gain)
    half = normed.shape[-1] // 2
    turned = jnp.concatenate([-normed[..., half:], normed[..., :half]], axis=-1)
    return normed * cosine + turned * sine


def dot_first(left, right):
    return lax.dot_general(
        left, right, (((0,), (0,)), ((), ())), preferred_element_type=jnp.float32
    )


def dot_last(left, right):
    return lax.dot_general(
        left, right, (((1,), (1,)), ((), ())), preferred_element_type=jnp.float32
    )


def project_rows(left, right):
    return jnp.dot(left, right, preferred_element_type=jnp.float32)


def project_pair(gate_back, gate_full, up_back, up_full):
    first_part = dot_last(gate_back, gate_full)
    return first_part + dot_last(up_back, up_full)


def project_three(query_back, query_full, key_back, key_full, value_back, value_full):
    total = dot_last(query_back, query_full)
    total = total + dot_last(key_back, key_full)
    return total + dot_last(value_back, value_full)


def fetch_weights(
    query_weight, key_weight, value_weight, output_weight, gate_weight, up_weight, down_weight
):
    return (
        lax.all_gather(query_weight, ("shard", "ctx"), axis=0, tiled=True),
        lax.all_gather(key_weight, ("shard", "ctx"), axis=0, tiled=True),
        lax.all_gather(value_weight, ("shard", "ctx"), axis=0, tiled=True),
        lax.all_gather(output_weight, ("shard", "ctx"), axis=1, tiled=True),
        lax.all_gather(gate_weight, ("shard", "ctx"), axis=0, tiled=True),
        lax.all_gather(up_weight, ("shard", "ctx"), axis=0, tiled=True),
        lax.all_gather(down_weight, ("shard", "ctx"), axis=1, tiled=True),
    )


def attend(query_b, key_b, value_b, first_query):
    span_rows, kv_heads, group, width = query_b.shape
    scale = 1.0 / math.sqrt(width)
    query_index = first_query + jnp.arange(span_rows)
    last_query = first_query + span_rows - 1
    init = (
        jnp.full((kv_heads, group, span_rows), NEGATIVE, jnp.float32),
        jnp.zeros((kv_heads, group, span_rows), jnp.float32),
        jnp.zeros((kv_heads, group, span_rows, width), jnp.float32),
    )
    key_piece = lax.all_gather(key_b, "ctx", axis=0, tiled=True)
    value_piece = lax.all_gather(value_b, "ctx", axis=0, tiled=True)

    def update(state):
        peak, total, accum = state
        scores = (
            jnp.einsum("qkgd,nkd->kgqn", query_b, key_piece, preferred_element_type=jnp.float32)
            * scale
        )
        key_index = jnp.arange(key_piece.shape[0])
        allowed = key_index[None, :] <= query_index[:, None]
        masked = jnp.where(allowed, scores, NEGATIVE)
        new_peak = jnp.maximum(peak, jnp.max(masked, axis=-1))
        weights = jnp.where(allowed, jnp.exp(masked - new_peak[..., None]), 0.0)
        total = jnp.sum(weights, axis=-1)
        accum = jnp.einsum(
            "kgqn,nkd->kgqd",
            weights.astype(jnp.bfloat16),
            value_piece,
            preferred_element_type=jnp.float32,
        )
        return (new_peak, total, accum)

    peak, total, accum = lax.cond(jnp.int32(0) <= last_query, update, lambda state: state, init)
    return (accum / total[..., None], peak + jnp.log(total))


def attend_back(query_b, keys_all, values_all, back_b, attention, logsum, first_query):
    span_rows, kv_heads, group, width = query_b.shape
    scale = 1.0 / math.sqrt(width)
    query_index = first_query + jnp.arange(span_rows)
    delta = jnp.einsum("qkgd,kgqd->kgq", back_b.astype(jnp.float32), attention)

    def block(index, carry):
        query_back, key_buffer, value_buffer = carry
        key_block = lax.dynamic_slice_in_dim(keys_all, index * span_rows, span_rows, 0)
        value_block = lax.dynamic_slice_in_dim(values_all, index * span_rows, span_rows, 0)
        scores = (
            jnp.einsum("qkgd,nkd->kgqn", query_b, key_block, preferred_element_type=jnp.float32)
            * scale
        )
        key_index = index * span_rows + jnp.arange(span_rows)
        allowed = key_index[None, :] <= query_index[:, None]
        probs = jnp.where(allowed, jnp.exp(scores - logsum[..., None]), 0.0)
        value_part = jnp.einsum(
            "kgqn,qkgd->nkd", probs.astype(jnp.bfloat16), back_b, preferred_element_type=jnp.float32
        )
        slopes = jnp.einsum(
            "qkgd,nkd->kgqn", back_b, value_block, preferred_element_type=jnp.float32
        )
        score_back = (probs * (slopes - delta[..., None])).astype(jnp.bfloat16)
        query_back = (
            query_back
            + jnp.einsum(
                "kgqn,nkd->qkgd", score_back, key_block, preferred_element_type=jnp.float32
            )
            * scale
        )
        key_part = (
            jnp.einsum("kgqn,qkgd->nkd", score_back, query_b, preferred_element_type=jnp.float32)
            * scale
        )
        key_buffer = lax.dynamic_update_slice_in_dim(key_buffer, key_part, index * span_rows, 0)
        value_buffer = lax.dynamic_update_slice_in_dim(
            value_buffer, value_part, index * span_rows, 0
        )
        return (query_back, key_buffer, value_buffer)

    init = (
        jnp.zeros(query_b.shape, jnp.float32),
        jnp.zeros(keys_all.shape, jnp.float32),
        jnp.zeros(values_all.shape, jnp.float32),
    )
    return lax.fori_loop(0, first_query // span_rows + 1, block, init)


def per_device(
    tokens,
    positions,
    first_gain,
    query_weight,
    key_weight,
    value_weight,
    query_gain,
    key_gain,
    output_weight,
    second_gain,
    gate_weight,
    up_weight,
    down_weight,
    upstream,
):
    sequences, rows, width = tokens.shape
    span_rows = positions.shape[1]
    head_dim = query_gain.shape[0]
    first_query = lax.axis_index("ctx") * span_rows
    query_acc = jnp.zeros((width, query_weight.shape[1]), jnp.float32)
    key_acc = jnp.zeros((width, key_weight.shape[1]), jnp.float32)
    value_acc = jnp.zeros((width, value_weight.shape[1]), jnp.float32)
    output_acc = jnp.zeros((output_weight.shape[0], width), jnp.float32)
    gate_acc = jnp.zeros((width, gate_weight.shape[1]), jnp.float32)
    up_acc = jnp.zeros((width, up_weight.shape[1]), jnp.float32)
    down_acc = jnp.zeros((down_weight.shape[0], width), jnp.float32)
    first_gain_acc = jnp.zeros_like(first_gain)
    second_gain_acc = jnp.zeros_like(second_gain)
    query_gain_acc = jnp.zeros_like(query_gain)
    key_gain_acc = jnp.zeros_like(key_gain)
    results = []
    gradients = []
    for seq in range(sequences):
        current = fetch_weights(
            query_weight,
            key_weight,
            value_weight,
            output_weight,
            gate_weight,
            up_weight,
            down_weight,
        )
        query_full, key_full, value_full, output_full, gate_full, up_full, down_full = current
        token_rows = tokens[seq].astype(jnp.float32)
        first = norm_rows(token_rows, first_gain).astype(jnp.bfloat16)
        first_all = lax.all_gather(first, "tp", axis=0, tiled=True)
        cosine, sine = rotary_tables(positions[seq], head_dim)
        query_raw = jnp.dot(first_all, query_full, preferred_element_type=jnp.float32).reshape(
            span_rows, -1, head_dim
        )
        key_raw = jnp.dot(first_all, key_full, preferred_element_type=jnp.float32).reshape(
            span_rows, -1, head_dim
        )
        value_b = (
            jnp.dot(first_all, value_full, preferred_element_type=jnp.float32)
            .astype(jnp.bfloat16)
            .reshape(span_rows, -1, head_dim)
        )
        kv_heads = key_raw.shape[1]
        group = query_raw.shape[1] // kv_heads

        def query_shape(raw, gain):
            return shape_heads(raw, gain, cosine, sine)

        query_b = (
            query_shape(query_raw, query_gain)
            .astype(jnp.bfloat16)
            .reshape(span_rows, kv_heads, group, head_dim)
        )
        key_b = query_shape(key_raw, key_gain).astype(jnp.bfloat16)
        attention, logsum = attend(query_b, key_b, value_b, first_query)
        mixed_b = jnp.transpose(attention, (2, 0, 1, 3)).reshape(span_rows, -1).astype(jnp.bfloat16)
        attn_rows = lax.psum_scatter(
            project_rows(mixed_b, output_full).astype(jnp.bfloat16),
            "tp",
            scatter_dimension=0,
            tiled=True,
        ).astype(jnp.float32)
        middle = token_rows + attn_rows
        second = norm_rows(middle, second_gain).astype(jnp.bfloat16)
        second_all = lax.all_gather(second, "tp", axis=0, tiled=True)
        gate = jnp.dot(second_all, gate_full, preferred_element_type=jnp.float32)
        up = jnp.dot(second_all, up_full, preferred_element_type=jnp.float32)
        gate_sig = jax.nn.sigmoid(gate)
        swish = gate * gate_sig
        hidden_b = (swish * up).astype(jnp.bfloat16)
        ffn_rows = lax.psum_scatter(
            project_rows(hidden_b, down_full).astype(jnp.bfloat16),
            "tp",
            scatter_dimension=0,
            tiled=True,
        ).astype(jnp.float32)
        results.append((middle + ffn_rows).astype(jnp.bfloat16))
        current = fetch_weights(
            query_weight,
            key_weight,
            value_weight,
            output_weight,
            gate_weight,
            up_weight,
            down_weight,
        )
        query_full, key_full, value_full, output_full, gate_full, up_full, down_full = current
        upstream_b = upstream[seq]
        upstream_all = lax.all_gather(upstream_b, "tp", axis=0, tiled=True)
        down_acc = down_acc + dot_first(hidden_b, upstream_all)
        hidden_back = dot_last(upstream_all, down_full)
        gate_back = (hidden_back * up * (gate_sig * (1.0 + gate * (1.0 - gate_sig)))).astype(
            jnp.bfloat16
        )
        up_back = (hidden_back * swish).astype(jnp.bfloat16)
        gate_acc = gate_acc + dot_first(second_all, gate_back)
        up_acc = up_acc + dot_first(second_all, up_back)
        second_back = lax.psum_scatter(
            project_pair(gate_back, gate_full, up_back, up_full).astype(jnp.bfloat16),
            "tp",
            scatter_dimension=0,
            tiled=True,
        ).astype(jnp.float32)
        unused_second, second_fn = jax.vjp(norm_rows, middle, second_gain)
        middle_part, second_part = second_fn(second_back)
        second_gain_acc = second_gain_acc + second_part
        middle_back = upstream_b.astype(jnp.float32) + middle_part
        mixed_back_all = lax.all_gather(middle_back.astype(jnp.bfloat16), "tp", axis=0, tiled=True)
        output_acc = output_acc + dot_first(mixed_b, mixed_back_all)
        attention_back = (
            dot_last(mixed_back_all, output_full)
            .astype(jnp.bfloat16)
            .reshape(span_rows, kv_heads, group, head_dim)
        )
        keys_all, values_all = (
            lax.all_gather(key_b, "ctx", axis=0, tiled=True),
            lax.all_gather(value_b, "ctx", axis=0, tiled=True),
        )
        query_back, key_buffer, value_buffer = attend_back(
            query_b, keys_all, values_all, attention_back, attention, logsum, first_query
        )
        key_back, value_back = (
            lax.psum_scatter(
                key_buffer.astype(jnp.bfloat16), "ctx", scatter_dimension=0, tiled=True
            ).astype(jnp.float32),
            lax.psum_scatter(
                value_buffer.astype(jnp.bfloat16), "ctx", scatter_dimension=0, tiled=True
            ).astype(jnp.float32),
        )
        value_back_b = value_back.reshape(span_rows, -1).astype(jnp.bfloat16)
        unused_key, key_fn = jax.vjp(query_shape, key_raw, key_gain)
        key_raw_back, key_gain_part = key_fn(key_back)
        unused_query, query_fn = jax.vjp(query_shape, query_raw, query_gain)
        query_raw_back, query_gain_part = query_fn(query_back.reshape(span_rows, -1, head_dim))
        key_raw_b = key_raw_back.reshape(span_rows, -1).astype(jnp.bfloat16)
        query_raw_b = query_raw_back.reshape(span_rows, -1).astype(jnp.bfloat16)
        key_gain_acc = key_gain_acc + key_gain_part
        query_gain_acc = query_gain_acc + query_gain_part
        query_acc = query_acc + dot_first(first_all, query_raw_b)
        key_acc = key_acc + dot_first(first_all, key_raw_b)
        value_acc = value_acc + dot_first(first_all, value_back_b)
        first_back = lax.psum_scatter(
            project_three(
                query_raw_b, query_full, key_raw_b, key_full, value_back_b, value_full
            ).astype(jnp.bfloat16),
            "tp",
            scatter_dimension=0,
            tiled=True,
        ).astype(jnp.float32)
        unused_first, first_fn = jax.vjp(norm_rows, token_rows, first_gain)
        token_part, first_part = first_fn(first_back)
        first_gain_acc = first_gain_acc + first_part
        gradients.append(middle_back + token_part)
    query_out, key_out, value_out, output_out, gate_out, up_out, down_out = (
        lax.psum_scatter(query_acc, ("shard", "ctx"), scatter_dimension=0, tiled=True),
        lax.psum_scatter(key_acc, ("shard", "ctx"), scatter_dimension=0, tiled=True),
        lax.psum_scatter(value_acc, ("shard", "ctx"), scatter_dimension=0, tiled=True),
        lax.psum_scatter(output_acc, ("shard", "ctx"), scatter_dimension=1, tiled=True),
        lax.psum_scatter(gate_acc, ("shard", "ctx"), scatter_dimension=0, tiled=True),
        lax.psum_scatter(up_acc, ("shard", "ctx"), scatter_dimension=0, tiled=True),
        lax.psum_scatter(down_acc, ("shard", "ctx"), scatter_dimension=1, tiled=True),
    )
    first_total, second_total, query_total, key_total = lax.psum(
        (first_gain_acc, second_gain_acc, query_gain_acc, key_gain_acc), ("shard", "ctx", "tp")
    )
    return (
        jnp.stack(results),
        jnp.stack(gradients),
        query_out,
        key_out,
        value_out,
        output_out,
        gate_out,
        up_out,
        down_out,
        first_total,
        second_total,
        query_total,
        key_total,
    )


def solution(mesh):
    in_specs = (
        P("shard", ("ctx", "tp"), None),
        P("shard", "ctx"),
        P(),
        P(("shard", "ctx"), "tp"),
        P(("shard", "ctx"), "tp"),
        P(("shard", "ctx"), "tp"),
        P(),
        P(),
        P("tp", ("shard", "ctx")),
        P(),
        P(("shard", "ctx"), "tp"),
        P(("shard", "ctx"), "tp"),
        P("tp", ("shard", "ctx")),
        P("shard", ("ctx", "tp"), None),
    )
    out_specs = (
        P("shard", ("ctx", "tp"), None),
        P("shard", ("ctx", "tp"), None),
        P(("shard", "ctx"), "tp"),
        P(("shard", "ctx"), "tp"),
        P(("shard", "ctx"), "tp"),
        P("tp", ("shard", "ctx")),
        P(("shard", "ctx"), "tp"),
        P(("shard", "ctx"), "tp"),
        P("tp", ("shard", "ctx")),
        P(),
        P(),
        P(),
        P(),
    )
    return jax.shard_map(
        per_device, mesh=mesh, in_specs=in_specs, out_specs=out_specs, check_vma=False
    )
```

profile of v0, /device:TPU:0, one launch (start us, length us, event | category | flops | bytes accessed | tf_op | source)
XLA Modules:
  0.0 1653.8 jit_solution(1743868269783206539)
XLA Ops:
  14.1 10.8 all_gather.39
  26.7 35.4 %all-gather.18.cloned.1.call-done = bf16[1024,1024]{1,0:T(8,128)(2,1)} async-done(((bf16[256,1024]{1,0:T(8,128)(2,1)}), bf16[1024,1024]{1,0:T(8,128)(2,1)}) %all-gather.18.cloned.1.call-update) | async-done | bytes 2097168 | tf_op jit(solution)/shard_map/all_gather | solution.py:204
  65.1 43.7 %all-gather.32.cloned.1.call-done = bf16[1024,1024]{1,0:T(8,128)(2,1)} async-done(((bf16[256,1024]{1,0:T(8,128)(2,1)}), bf16[1024,1024]{1,0:T(8,128)(2,1)}) %all-gather.32.cloned.1.call-update) | async-done | bytes 2097168 | tf_op jit(solution)/shard_map/all_gather | solution.py:204
  114.0 9.6 all_gather.42
  125.2 10.8 all_gather.41
  140.3 12.0 all_gather.88
  164.3 84.7 %conditional.2 = (f32[2,2,1024]{2,1,0:T(2,128)}, f32[2,2,1024]{2,1,0:T(2,128)}, f32[2,2,1024,64]{2,3,1,0:T(8,128)S(1)}, f32[2,2,1024]{2,1,0:T(2,128)S(1)}) conditional(s32[]{:T(128)} %convert_element_type.260, () %tuple.36, (s32[1024]{0:T(1024)S(1)}, bf16[4096,2,64]{0,2,1:T(8,128)(2,1)}, bf16[1024,2,2,64]{0,3,2,1:T(8,128)(2,1)}, ...), branch_computations={%region_3.0_spmd, %region_4.7_spmd} | conditional | flops 4517261312 | bytes 226103360 | solution.py:105
  170.2 27.5 %fusion.4 = (f32[2,2,1024]{2,1,0:T(2,128)S(1)}, f32[2,4096,1024,2]{2,1,3,0:T(8,128)}) fusion(pred[1024,4096]{0,1:T(8,128)(4,1)} %iota_compare_fusion, bf16[1024,2,2,64]{0,3,2,1:T(8,128)(2,1)} %get-tuple-element.116, bf16[4096,2,64]{0,2,1:T(8,128)(2,1)} %get-tuple-element.115), kind=kOutput, calls=%fused_computation.4 | convolution fusion | flops 2197811200 | bytes 72892416 | tf_op jit(solution)/shard_map/cond/branch_1_fun/qkgd,nkd->kgqn/dot_general | solution.py:88
  198.3 23.9 %fusion.6 = f32[2,2,1024]{2,1,0:T(2,128)} fusion(f32[2,4096,1024,2]{2,1,3,0:T(8,128)} %get-tuple-element.326, f32[2,2,1024]{2,1,0:T(2,128)} %broadcast_maximum_fusion, pred[1024,4096]{0,1:T(8,128)(4,1)} %iota_compare_fusion), kind=kLoop, calls=%fused_computation.6 | loop fusion | flops 83881984 | bytes 71335936 | tf_op jit(solution)/shard_map/cond/branch_1_fun/reduce_sum | solution.py:96
  222.2 26.1 %fusion.7 = f32[2,2,1024,64]{2,3,1,0:T(8,128)S(1)} fusion(f32[2,4096,1024,2]{2,1,3,0:T(8,128)} %get-tuple-element.326, f32[2,2,1024]{2,1,0:T(2,128)} %broadcast_maximum_fusion, pred[1024,4096]{0,1:T(8,128)(4,1)} %iota_compare_fusion, bf16[4096,2,64]{0,2,1:T(8,128)(2,1)S(1)} %copy-done.129), kind=kOutput, calls=%fused_computation.7 | convolution fusion | flops 2231369728 | bytes 73416704 | tf_op jit(solution)/shard_map/cond/branch_1_fun/kgqn,nkd->kgqd/dot_general | solution.py:97
  252.9 83.4 %conditional.3 = (f32[2,2,1024]{2,1,0:T(2,128)}, f32[2,2,1024]{2,1,0:T(2,128)}, f32[2,2,1024,64]{2,3,1,0:T(8,128)S(1)}, f32[2,2,1024]{2,1,0:T(2,128)S(1)}) conditional(s32[]{:T(128)} %convert_element_type.260, () %tuple.38, (s32[1024]{0:T(1024)S(1)}, bf16[4096,2,64]{0,2,1:T(8,128)(2,1)}, bf16[1024,2,2,64]{0,3,2,1:T(8,128)(2,1)S(1)}, ...), branch_computations={%region_13.14_spmd, %region_14.17_spmd} | conditional | flops 4517261312 | bytes 230297696 | solution.py:105
  258.8 25.9 %fusion.16 = (f32[2,2,1024]{2,1,0:T(2,128)S(1)}, f32[2,4096,1024,2]{2,1,3,0:T(8,128)}) fusion(pred[1024,4096]{0,1:T(8,128)(4,1)} %iota_compare_fusion.1, bf16[1024,2,2,64]{0,3,2,1:T(8,128)(2,1)S(1)} %get-tuple-element.120, bf16[4096,2,64]{0,2,1:T(8,128)(2,1)S(1)} %copy-done.37), kind=kOutput, calls=%fused_computation.19 | convolution fusion | flops 2197811200 | bytes 72892416 | tf_op jit(solution)/shard_map/cond/branch_1_fun/qkgd,nkd->kgqn/dot_general | solution.py:88
  285.4 24.1 %fusion.18 = f32[2,2,1024]{2,1,0:T(2,128)} fusion(f32[2,4096,1024,2]{2,1,3,0:T(8,128)} %get-tuple-element.328, f32[2,2,1024]{2,1,0:T(2,128)} %broadcast_maximum_fusion.1, pred[1024,4096]{0,1:T(8,128)(4,1)} %iota_compare_fusion.1), kind=kLoop, calls=%fused_computation.21 | loop fusion | flops 83881984 | bytes 71335936 | tf_op jit(solution)/shard_map/cond/branch_1_fun/reduce_sum | solution.py:96
  309.4 26.1 %fusion.19 = f32[2,2,1024,64]{2,3,1,0:T(8,128)S(1)} fusion(f32[2,4096,1024,2]{2,1,3,0:T(8,128)} %get-tuple-element.328, f32[2,2,1024]{2,1,0:T(2,128)} %broadcast_maximum_fusion.1, pred[1024,4096]{0,1:T(8,128)(4,1)} %iota_compare_fusion.1, bf16[4096,2,64]{0,2,1:T(8,128)(2,1)S(1)} %copy-done.128), kind=kOutput, calls=%fused_computation.22 | convolution fusion | flops 2231369728 | bytes 73416704 | tf_op jit(solution)/shard_map/cond/branch_1_fun/kgqn,nkd->kgqd/dot_general | solution.py:97
  340.0 42.3 %reduce-scatter.24.cloned.1.call-done = bf16[256,1024]{1,0:T(8,128)(2,1)} async-done(((bf16[1024,1024]{1,0:T(8,128)(2,1)}), bf16[256,1024]{1,0:T(8,128)(2,1)}) %reduce-scatter.24.cloned.1.call-update) | async-done | bytes 524304 | tf_op jit(solution)/shard_map/reduce_scatter | solution.py:231
  391.0 40.7 %all-gather.24.cloned.1.call-done = bf16[1024,1024]{1,0:T(8,128)(2,1)} async-done(((bf16[256,1024]{1,0:T(8,128)(2,1)}), bf16[1024,1024]{1,0:T(8,128)(2,1)}) %all-gather.24.cloned.1.call-update) | async-done | bytes 2097168 | tf_op jit(solution)/shard_map/all_gather | solution.py:239
  439.1 22.1 %all-gather.28.cloned.1.call-done = bf16[1024,1152]{1,0:T(8,128)(2,1)} async-done(((bf16[128,1152]{1,0:T(8,128)(2,1)}), bf16[1024,1152]{1,0:T(8,128)(2,1)}) %all-gather.28.cloned.1.call-update) | async-done | bytes 2359312 | tf_op jit(solution)/shard_map/all_gather | solution.py:67
  468.6 40.3 %all-gather.44.cloned.1.call-done = bf16[1,1024,1024]{2,1,0:T(8,128)(2,1)} async-done(((bf16[1,256,1024]{2,1,0:T(8,128)(2,1)}), bf16[1,1024,1024]{2,1,0:T(8,128)(2,1)}) %all-gather.44.cloned.1.call-update) | async-done | bytes 2097168 | tf_op jit(solution)/shard_map/all_gather | solution.py:263
  508.9 29.9 %all-gather.30.cloned.1.call-done = bf16[1152,1024]{1,0:T(8,128)(2,1)} async-done(((bf16[1152,128]{1,0:T(8,128)(2,1)}), bf16[1152,1024]{1,0:T(8,128)(2,1)}) %all-gather.30.cloned.1.call-update) | async-done | bytes 2359312 | tf_op jit(solution)/shard_map/all_gather | solution.py:68
  538.8 10.8 multiply_convert_fusion.2
  557.4 49.3 %all-gather.38.cloned.1.call-done = bf16[1024,1024]{1,0:T(8,128)(2,1)} async-done(((bf16[256,1024]{1,0:T(8,128)(2,1)}), bf16[1024,1024]{1,0:T(8,128)(2,1)}) %all-gather.38.cloned.1.call-update) | async-done | bytes 2097168 | tf_op jit(solution)/shard_map/all_gather | solution.py:239
  618.6 36.3 %all-gather.46.cloned.1.call-done = bf16[1,1024,1024]{2,1,0:T(8,128)(2,1)} async-done(((bf16[1,256,1024]{2,1,0:T(8,128)(2,1)}), bf16[1,1024,1024]{2,1,0:T(8,128)(2,1)}) %all-gather.46.cloned.1.call-update) | async-done | bytes 2097168 | tf_op jit(solution)/shard_map/all_gather | solution.py:263
  654.9 10.9 multiply_convert_fusion
  680.7 35.6 %reduce-scatter.36.cloned.1.call-done = bf16[256,1024]{1,0:T(8,128)(2,1)} async-done(((bf16[1024,1024]{1,0:T(8,128)(2,1)}), bf16[256,1024]{1,0:T(8,128)(2,1)}) %reduce-scatter.36.cloned.1.call-update) | async-done | bytes 524304 | tf_op jit(solution)/shard_map/reduce_scatter | solution.py:272
  719.1 42.7 %reduce-scatter.26.cloned.1.call-done = bf16[256,1024]{1,0:T(8,128)(2,1)} async-done(((bf16[1024,1024]{1,0:T(8,128)(2,1)}), bf16[256,1024]{1,0:T(8,128)(2,1)}) %reduce-scatter.26.cloned.1.call-update) | async-done | bytes 524304 | tf_op jit(solution)/shard_map/reduce_scatter | solution.py:245
  767.1 43.3 %all-gather.40.cloned.1.call-done = bf16[1024,1024]{1,0:T(8,128)(2,1)} async-done(((bf16[256,1024]{1,0:T(8,128)(2,1)}), bf16[1024,1024]{1,0:T(8,128)(2,1)}) %all-gather.40.cloned.1.call-update) | async-done | bytes 2097168 | tf_op jit(solution)/shard_map/all_gather | solution.py:282
  815.4 35.1 %while.30 = (s32[]{:T(128)}, f32[1024,2,2,64]{0,3,2,1:T(8,128)S(1)}, bf16[4096,2,64]{0,2,1:T(8,128)(2,1)}, bf16[4096,2,64]{0,2,1:T(8,128)(2,1)}, s32[]{:T(128)},...) while((s32[]{:T(128)}, ...), condition=%wide.region_23.24_spmd.clone, body=%wide.region_22.23_spmd.clone.sunk | while | flops 2728003584 | bytes 93126936 | solution.py:155
  815.4 9.3 fusion.318
  825.4 9.2 fusion.319
  842.1 8.4 fusion.322
  862.6 34.7 %while.31 = (s32[]{:T(128)}, f32[1024,2,2,64]{0,3,2,1:T(8,128)S(1)}, bf16[4096,2,64]{0,2,1:T(8,128)(2,1)}, bf16[4096,2,64]{0,2,1:T(8,128)(2,1)}, s32[]{:T(128)},...) while((s32[]{:T(128)}, ...), condition=%wide.region_33.34_spmd.clone, body=%wide.region_32.33_spmd.clone.sunk | while | flops 2728003584 | bytes 99418456 | solution.py:155
  862.8 9.2 fusion.333
  872.7 9.5 fusion.334
  888.7 8.6 fusion.337
  910.4 68.9 %reduce-scatter.30.cloned.1.call-done = bf16[1024,2,64]{0,2,1:T(8,128)(2,1)} async-done(((bf16[4096,2,64]{0,2,1:T(8,128)(2,1)}), bf16[1024,2,64]{0,2,1:T(8,128)(2,1)}) %reduce-scatter.30.cloned.1.call-update) | async-done | bytes 262160 | tf_op jit(solution)/shard_map/reduce_scatter | solution.py:297
  980.5 142.9 %reduce-scatter.38.cloned.1.call-done = bf16[1024,2,64]{0,2,1:T(8,128)(2,1)} async-done(((bf16[4096,2,64]{0,2,1:T(8,128)(2,1)}), bf16[1024,2,64]{0,2,1:T(8,128)(2,1)}) %reduce-scatter.38.cloned.1.call-update) | async-done | bytes 262160 | tf_op jit(solution)/shard_map/reduce_scatter | solution.py:297
  1130.6 20.8 %reduce-scatter.32.cloned.1.call-done = bf16[1024,2,64]{0,2,1:T(8,128)(2,1)} async-done(((bf16[4096,2,64]{0,2,1:T(8,128)(2,1)}), bf16[1024,2,64]{0,2,1:T(8,128)(2,1)}) %reduce-scatter.32.cloned.1.call-update) | async-done | bytes 262160 | tf_op jit(solution)/shard_map/reduce_scatter | solution.py:300
  1162.8 16.0 reduce-scatter.40.cloned.1.call-done
  1238.9 31.9 %reduce-scatter.42.cloned.1.call-done = bf16[256,1024]{1,0:T(8,128)(2,1)} async-done(((bf16[1024,1024]{1,0:T(8,128)(2,1)}), bf16[256,1024]{1,0:T(8,128)(2,1)}) %reduce-scatter.42.cloned.1.call-update) | async-done | bytes 524304 | tf_op jit(solution)/shard_map/reduce_scatter | solution.py:316
  1273.0 43.3 %reduce-scatter.22.cloned.1.call-done = bf16[256,1024]{1,0:T(8,128)(2,1)} async-done(((bf16[1024,1024]{1,0:T(8,128)(2,1)}), bf16[256,1024]{1,0:T(8,128)(2,1)}) %reduce-scatter.22.cloned.1.call-update) | async-done | bytes 524304 | tf_op jit(solution)/shard_map/reduce_scatter | solution.py:245
  1319.6 39.9 %all-reduce.8 = (f32[1024]{0:T(1024)}, f32[1024]{0:T(1024)}, f32[64]{0:T(128)}, f32[64]{0:T(128)}) all-reduce(f32[1024]{0:T(1024)S(1)} %add.369, f32[1024]{0:T(1024)S(1)} %add.370, f32[64]{0:T(128)S(1)} %add.371, f32[64]{0:T(128)S(1)} %add.372), channel_id=1, replica_groups=mesh['shard'=2,'ctx'=4,'tp'=4] {'shard','ctx','tp'}, use_global_device_ids=true, to_apply=%region_49.50 | all-reduce | flops 2176 | bytes 17408 | tf_op jit(solution)/shard_map/psum | solution.py:337
  1365.2 9.0 reduce-scatter.52.cloned.1.call-done
  1374.2 58.2 %reduce-scatter.54.cloned.1.call-done = f32[128,1152]{1,0:T(8,128)} async-done(((f32[1024,1152]{1,0:T(8,128)}), f32[128,1152]{1,0:T(8,128)}) %reduce-scatter.54.cloned.1.call-update) | async-done | bytes 589840 | tf_op jit(solution)/shard_map/reduce_scatter | solution.py:334
  1432.3 57.9 %reduce-scatter.56.cloned.1.call-done = f32[1152,128]{1,0:T(8,128)} async-done(((f32[1152,1024]{1,0:T(8,128)}), f32[1152,128]{1,0:T(8,128)}) %reduce-scatter.56.cloned.1.call-update) | async-done | bytes 589840 | tf_op jit(solution)/shard_map/reduce_scatter | solution.py:335
  1490.3 40.1 %reduce-scatter.44.cloned.1.call-done = f32[128,256]{1,0:T(8,128)} async-done(((f32[1024,256]{1,0:T(8,128)}), f32[128,256]{1,0:T(8,128)}) %reduce-scatter.44.cloned.1.call-update) | async-done | bytes 131088 | tf_op jit(solution)/shard_map/reduce_scatter | solution.py:329
  1530.4 40.1 %reduce-scatter.50.cloned.1.call-done = f32[256,128]{1,0:T(8,128)} async-done(((f32[256,1024]{1,0:T(8,128)}), f32[256,128]{1,0:T(8,128)}) %reduce-scatter.50.cloned.1.call-update) | async-done | bytes 131088 | tf_op jit(solution)/shard_map/reduce_scatter | solution.py:332
  1570.5 37.9 %reduce-scatter.46.cloned.1.call-done = f32[128,128]{1,0:T(8,128)} async-done(((f32[1024,128]{1,0:T(8,128)}), f32[128,128]{1,0:T(8,128)}) %reduce-scatter.46.cloned.1.call-update) | async-done | bytes 65552 | tf_op jit(solution)/shard_map/reduce_scatter | solution.py:330
  1608.5 37.7 %reduce-scatter.48.cloned.1.call-done = f32[128,128]{1,0:T(8,128)} async-done(((f32[1024,128]{1,0:T(8,128)}), f32[128,128]{1,0:T(8,128)}) %reduce-scatter.48.cloned.1.call-update) | async-done | bytes 65552 | tf_op jit(solution)/shard_map/reduce_scatter | solution.py:331
  (477 shorter events, 256.3 us)
Async XLA Ops:
  8.0 54.0 %all-gather.18.cloned.1.call-start = ((), (), s32[]{:S(2)}) async-start(), calls=%async_computation.19 | async-start | bytes 2621440 | tf_op jit(solution)/shard_map/all_gather | solution.py:204
  13.3 95.5 %all-gather.32.cloned.1.call-start = ((), (), s32[]{:S(2)}) async-start(), calls=%async_computation.28 | async-start | bytes 2621440 | tf_op jit(solution)/shard_map/all_gather | solution.py:204
  14.0 150.3 %all-gather.20.cloned.1.call-start = ((), (), s32[]{:S(2)}) async-start(), calls=%async_computation.20 | async-start | bytes 1310720 | tf_op jit(solution)/shard_map/all_gather | solution.py:82
  113.9 50.4 %all-gather.22.cloned.1.call-start = ((), (), s32[]{:S(2)}) async-start(), calls=%async_computation.21 | async-start | bytes 1310720 | tf_op jit(solution)/shard_map/all_gather | solution.py:83
  125.2 127.7 %all-gather.34.cloned.1.call-start = ((), (), s32[]{:S(2)}) async-start(), calls=%async_computation.29 | async-start | bytes 1310720 | tf_op jit(solution)/shard_map/all_gather | solution.py:82
  140.2 112.7 %all-gather.36.cloned.1.call-start = ((), (), s32[]{:S(2)}) async-start(), calls=%async_computation.30 | async-start | bytes 1310720 | tf_op jit(solution)/shard_map/all_gather | solution.py:83
  156.7 183.3 %reduce-scatter.20.cloned.1.call-start = ((), (), s32[]{:S(2)}) async-start(), calls=%async_computation.22 | async-start | bytes 2621440 | tf_op jit(solution)/shard_map/reduce_scatter | solution.py:231
  252.6 129.7 %reduce-scatter.24.cloned.1.call-start = ((), (), s32[]{:S(2)}) async-start(), calls=%async_computation.31 | async-start | bytes 2621440 | tf_op jit(solution)/shard_map/reduce_scatter | solution.py:231
  339.4 51.6 %all-gather.26.cloned.1.call-start = ((), (), s32[]{:S(2)}) async-start(), calls=%async_computation.24 | async-start | bytes 2654208 | tf_op jit(solution)/shard_map/all_gather | solution.py:66
  340.0 91.8 %all-gather.24.cloned.1.call-start = ((), (), s32[]{:S(2)}) async-start(), calls=%async_computation.23 | async-start | bytes 2621440 | tf_op jit(solution)/shard_map/all_gather | solution.py:239
  384.0 377.8 %copy-start.96 = (f32[256]{0:T(256)}, f32[256]{0:T(256)S(1)}, u32[]{:S(2)}) copy-start(f32[256]{0:T(256)S(1)} %fusion.156) | copy-start | bytes 3076
  384.0 377.8 %copy-start.94 = (f32[256]{0:T(256)}, f32[256]{0:T(256)S(1)}, u32[]{:S(2)}) copy-start(f32[256]{0:T(256)S(1)} %fusion.158) | copy-start | bytes 3076
  386.7 74.4 %all-gather.28.cloned.1.call-start = ((), (), s32[]{:S(2)}) async-start(), calls=%async_computation.25 | async-start | bytes 2654208 | tf_op jit(solution)/shard_map/all_gather | solution.py:67
  387.3 121.6 %all-gather.44.cloned.1.call-start = ((), (), s32[]{:S(2)}) async-start(), calls=%async_computation.51 | async-start | bytes 2621440 | tf_op jit(solution)/shard_map/all_gather | solution.py:263
  388.4 150.4 %all-gather.30.cloned.1.call-start = ((), (), s32[]{:S(2)}) async-start(), calls=%async_computation.26 | async-start | bytes 2654208 | tf_op jit(solution)/shard_map/all_gather | solution.py:68
  389.2 217.5 %all-gather.38.cloned.1.call-start = ((), (), s32[]{:S(2)}) async-start(), calls=%async_computation.32 | async-start | bytes 2621440 | tf_op jit(solution)/shard_map/all_gather | solution.py:239
  389.9 265.0 %all-gather.46.cloned.1.call-start = ((), (), s32[]{:S(2)}) async-start(), calls=%async_computation.52 | async-start | bytes 2621440 | tf_op jit(solution)/shard_map/all_gather | solution.py:263
  390.5 290.2 %reduce-scatter.28.cloned.1.call-start = ((), (), s32[]{:S(2)}) async-start(), calls=%async_computation.34 | async-start | bytes 2621440 | tf_op jit(solution)/shard_map/reduce_scatter | solution.py:272
  557.1 159.1 %reduce-scatter.36.cloned.1.call-start = ((), (), s32[]{:S(2)}) async-start(), calls=%async_computation.39 | async-start | bytes 2621440 | tf_op jit(solution)/shard_map/reduce_scatter | solution.py:272
  673.4 88.4 %reduce-scatter.26.cloned.1.call-start = ((), (), s32[]{:S(2)}) async-start(), calls=%async_computation.33 | async-start | bytes 2621440 | tf_op jit(solution)/shard_map/reduce_scatter | solution.py:245
  680.2 130.2 %all-gather.40.cloned.1.call-start = ((), (), s32[]{:S(2)}) async-start(), calls=%async_computation.35 | async-start | bytes 2621440 | tf_op jit(solution)/shard_map/all_gather | solution.py:282
  765.4 91.4 %all-gather.42.cloned.1.call-start = ((), (), s32[]{:S(2)}) async-start(), calls=%async_computation.40 | async-start | bytes 2621440 | tf_op jit(solution)/shard_map/all_gather | solution.py:282
  767.0 212.3 %reduce-scatter.30.cloned.1.call-start = ((), (), s32[]{:S(2)}) async-start(), calls=%async_computation.36 | async-start | bytes 1310720 | tf_op jit(solution)/shard_map/reduce_scatter | solution.py:297
  850.6 272.8 %reduce-scatter.38.cloned.1.call-start = ((), (), s32[]{:S(2)}) async-start(), calls=%async_computation.41 | async-start | bytes 1310720 | tf_op jit(solution)/shard_map/reduce_scatter | solution.py:297
  897.3 254.2 %reduce-scatter.32.cloned.1.call-start = ((), (), s32[]{:S(2)}) async-start(), calls=%async_computation.37 | async-start | bytes 1310720 | tf_op jit(solution)/shard_map/reduce_scatter | solution.py:300
  900.8 278.0 %reduce-scatter.40.cloned.1.call-start = ((), (), s32[]{:S(2)}) async-start(), calls=%async_computation.42 | async-start | bytes 1310720 | tf_op jit(solution)/shard_map/reduce_scatter | solution.py:300
  907.5 215.9 %copy-start.46 = (f32[1024,64]{0,1:T(8,128)S(1)}, f32[1024,64]{0,1:T(8,128)}, u32[]{:S(2)}) copy-start(f32[1024,64]{0,1:T(8,128)} %copy-done.45) | copy-start | bytes 786436
  907.5 217.1 %copy-start.18 = (f32[1024,128]{0,1:T(8,128)S(1)}, f32[1024,128]{0,1:T(8,128)}, u32[]{:S(2)}) copy-start(f32[1024,128]{0,1:T(8,128)} %copy-done.17) | copy-start | bytes 1572868
  907.5 217.1 %copy-start.20 = (f32[1024,128]{0,1:T(8,128)S(1)}, f32[1024,128]{0,1:T(8,128)}, u32[]{:S(2)}) copy-start(f32[1024,128]{0,1:T(8,128)} %copy-done.19) | copy-start | bytes 1572868
  907.5 217.1 %copy-start.31 = (f32[1024,64]{0,1:T(8,128)S(1)}, f32[1024,64]{0,1:T(8,128)}, u32[]{:S(2)}) copy-start(f32[1024,64]{0,1:T(8,128)} %copy-done.28) | copy-start | bytes 786436
  907.5 217.1 %copy-start.81 = (f32[1024,2]{0,1:T(2,128)S(1)}, f32[1024,2]{0,1:T(2,128)}, u32[]{:S(2)}) copy-start(f32[1024,2]{0,1:T(2,128)} %copy-done.80) | copy-start | bytes 24580
  907.5 217.1 %copy-start.83 = (f32[1024,2]{0,1:T(2,128)S(1)}, f32[1024,2]{0,1:T(2,128)}, u32[]{:S(2)}) copy-start(f32[1024,2]{0,1:T(2,128)} %copy-done.82) | copy-start | bytes 24580
  907.5 217.1 %copy-start.116 = (f32[64]{0:T(128)S(1)}, f32[64]{0:T(128)}, u32[]{:S(2)}) copy-start(f32[64]{0:T(128)} %param.29) | copy-start | bytes 772
  910.4 215.8 %copy-start.87 = (f32[1024,2]{0,1:T(2,128)S(1)}, f32[1024,2]{0,1:T(2,128)}, u32[]{:S(2)}) copy-start(f32[1024,2]{0,1:T(2,128)} %copy-done.86) | copy-start | bytes 24580
  910.4 215.9 %copy-start.89 = (f32[1024,2]{0,1:T(2,128)S(1)}, f32[1024,2]{0,1:T(2,128)}, u32[]{:S(2)}) copy-start(f32[1024,2]{0,1:T(2,128)} %copy-done.88) | copy-start | bytes 24580
  910.4 328.5 %reduce-scatter.34.cloned.1.call-start = ((), (), s32[]{:S(2)}) async-start(), calls=%async_computation.38 | async-start | bytes 2621440 | tf_op jit(solution)/shard_map/reduce_scatter | solution.py:316
  979.4 145.3 %copy-start.65 = (bf16[1024,2,64]{0,2,1:T(8,128)(2,1)S(1)}, bf16[1024,2,64]{0,2,1:T(8,128)(2,1)}, u32[]{:S(2)}) copy-start(bf16[1024,2,64]{0,2,1:T(8,128)(2,1)} %reduce-scatter.30.cloned.1.call-done) | copy-start | bytes 786436
  980.5 145.8 %copy-start.67 = (f32[1024,2,32]{0,2,1:T(8,128)}, f32[1024,2,32]{0,2,1:T(8,128)S(1)}, u32[]{:S(2)}) copy-start(f32[1024,2,32]{0,2,1:T(8,128)S(1)} %get-tuple-element.358) | copy-start | bytes 786436
  980.5 145.8 %copy-start.68 = (f32[1024,2,32]{0,2,1:T(8,128)}, f32[1024,2,32]{0,2,1:T(8,128)S(1)}, u32[]{:S(2)}) copy-start(f32[1024,2,32]{0,2,1:T(8,128)S(1)} %get-tuple-element.359) | copy-start | bytes 786436
  1157.2 113.7 %reduce-scatter.42.cloned.1.call-start = ((), (), s32[]{:S(2)}) async-start(), calls=%async_computation.43 | async-start | bytes 2621440 | tf_op jit(solution)/shard_map/reduce_scatter | solution.py:316
  1184.4 131.9 %reduce-scatter.22.cloned.1.call-start = ((), (), s32[]{:S(2)}) async-start(), calls=%async_computation.27 | async-start | bytes 2621440 | tf_op jit(solution)/shard_map/reduce_scatter | solution.py:245
  1191.2 183.0 %reduce-scatter.52.cloned.1.call-start = ((), (), s32[]{:S(2)}) async-start(), calls=%async_computation.48 | async-start | bytes 5308416 | tf_op jit(solution)/shard_map/reduce_scatter | solution.py:333
  1201.3 231.0 %reduce-scatter.54.cloned.1.call-start = ((), (), s32[]{:S(2)}) async-start(), calls=%async_computation.49 | async-start | bytes 5308416 | tf_op jit(solution)/shard_map/reduce_scatter | solution.py:334
  1211.0 279.3 %reduce-scatter.56.cloned.1.call-start = ((), (), s32[]{:S(2)}) async-start(), calls=%async_computation.50 | async-start | bytes 5308416 | tf_op jit(solution)/shard_map/reduce_scatter | solution.py:335
  1221.4 309.0 %reduce-scatter.44.cloned.1.call-start = ((), (), s32[]{:S(2)}) async-start(), calls=%async_computation.44 | async-start | bytes 1179648 | tf_op jit(solution)/shard_map/reduce_scatter | solution.py:329
  1227.6 342.9 %reduce-scatter.50.cloned.1.call-start = ((), (), s32[]{:S(2)}) async-start(), calls=%async_computation.47 | async-start | bytes 1179648 | tf_op jit(solution)/shard_map/reduce_scatter | solution.py:332
  1231.9 376.6 %reduce-scatter.46.cloned.1.call-start = ((), (), s32[]{:S(2)}) async-start(), calls=%async_computation.45 | async-start | bytes 589824 | tf_op jit(solution)/shard_map/reduce_scatter | solution.py:330
  1235.5 410.7 %reduce-scatter.48.cloned.1.call-start = ((), (), s32[]{:S(2)}) async-start(), calls=%async_computation.46 | async-start | bytes 589824 | tf_op jit(solution)/shard_map/reduce_scatter | solution.py:331
  (123 other events, 2753.7 us)
Sparse Core Ops, SparseCore 0:
  13.4 48.6 all-gather.17
  64.2 44.5 all-gather.31
  114.1 15.5 all-gather.19
  131.7 17.8 all-gather.21
  151.0 17.9 all-gather.33
  170.4 16.7 all-gather.35
  252.7 42.6 reduce-scatter.19
  339.5 42.7 reduce-scatter.23
  557.2 63.3 reduce-scatter.27
  673.6 42.6 reduce-scatter.35
  718.6 43.1 reduce-scatter.25
  850.7 128.6 reduce-scatter.29
  981.9 141.4 reduce-scatter.37
  1126.5 24.8 reduce-scatter.31
  1153.8 24.8 reduce-scatter.39
  1181.6 43.8 reduce-scatter.33
  1227.6 43.1 reduce-scatter.41
  1273.1 43.1 reduce-scatter.21
  1320.3 53.8 reduce-scatter.51
  1378.4 53.8 reduce-scatter.53
  1436.4 53.8 reduce-scatter.55
  1494.3 36.0 reduce-scatter.43
  1534.5 35.9 reduce-scatter.49
  1574.3 34.0 reduce-scatter.45
  1612.1 34.0 reduce-scatter.47
Sparse Core Ops, SparseCore 1:
  341.7 27.7 all-gather.25
  386.8 44.9 all-gather.23
  433.5 27.6 all-gather.27
  463.3 45.5 all-gather.43
  510.8 28.0 all-gather.29
  541.1 65.5 all-gather.37
  608.1 46.7 all-gather.45
  765.5 44.8 all-gather.39
  812.4 44.3 all-gather.41
where the time goes:
time: 1660 us; the launch traced here: 1650 us
  waiting for transfers between devices  1080 us (65%)
  matrix products  331 us (20%)
  other arithmetic  120 us (7%)
  blocking collectives  83.1 us (5%)
  local copies, waits for them, and re-layouts  20 us (1%)
  between operations  17.8 us (1%)
    reduce_scatter x2, waiting for transfers between devices, per_device(): lax.psum_scatter(key_buffer.astype(jnp.bfloat16), 'ctx', scatter_dimensio...  212 us
    all_gather x2, waiting for transfers between devices, per_device(): second_all = lax.all_gather(second, 'tp', axis=0, tiled=True)  90 us
    reduce_scatter x2, waiting for transfers between devices, per_device(): lax.psum_scatter(project_rows(hidden_b, down_full).astype(jnp.bfloat16),...  86 us
    all_gather x2, waiting for transfers between devices, per_device(): first_all = lax.all_gather(first, 'tp', axis=0, tiled=True)  79.1 us
    all_gather x2, waiting for transfers between devices, per_device(): upstream_all = lax.all_gather(upstream_b, 'tp', axis=0, tiled=True)  76.7 us
    dot_general x14, matrix products, dot_last(): lax.dot_general(left, right, (((1,), (1,)), ((), ())), preferred_element_...  64.4 us
    reduce_scatter x1, waiting for transfers between devices, per_device(): lax.psum_scatter(up_acc, ('shard', 'ctx'), scatter_dimension=0, tiled=True)  58.2 us
    reduce_scatter x1, waiting for transfers between devices, per_device(): lax.psum_scatter(down_acc, ('shard', 'ctx'), scatter_dimension=1, tiled=T...  57.9 us
  transfers between devices with their start and end apart: 34, of which 26 were waited for; matrix products, arithmetic and copies ran while one was open for 27% of the time, Pallas kernels for 0%

commit v1 on v0

--- a/solution.py
+++ b/solution.py
@@ -7,6 +7,24 @@
 EPS = 1e-05
 THETA = 1000000.0
 NEGATIVE = -1e30
+
+
+def in_order(tiles, dim):
+    dims = list(tiles.shape[1:])
+    dims[dim] *= tiles.shape[0]
+    return jnp.moveaxis(tiles, 0, dim).reshape(dims)
+
+
+def collected_by_bits(shard, axis):
+    size = lax.axis_size(axis)
+    blocks = shard[None]
+    for level in range(size.bit_length() - 1):
+        bit = 1 << level
+        partner_block = lax.ppermute(blocks, axis, [(i, i ^ bit) for i in range(size)])
+        both = jnp.stack([blocks, partner_block])
+        upper = lax.axis_index(axis) >> level & 1
+        blocks = jnp.where(upper == 0, both, both[::-1]).reshape(-1, *shard.shape)
+    return blocks
 
 
 def norm_rows(values, gain):
@@ -201,7 +219,7 @@
         query_full, key_full, value_full, output_full, gate_full, up_full, down_full = current
         token_rows = tokens[seq].astype(jnp.float32)
         first = norm_rows(token_rows, first_gain).astype(jnp.bfloat16)
-        first_all = lax.all_gather(first, "tp", axis=0, tiled=True)
+        first_all = in_order(collected_by_bits(first, "tp"), 0)
         cosine, sine = rotary_tables(positions[seq], head_dim)
         query_raw = jnp.dot(first_all, query_full, preferred_element_type=jnp.float32).reshape(
             span_rows, -1, head_dim

time: 1660 us -> 1700 us (1.024)
    ppermute x0 -> x4, waiting for transfers between devices: none -> 83.2 us  [collected_by_bits(): lax.ppermute(blocks, axis, [(i, i ^ bit) for i in range(size)])]
    all_gather x2 -> x0, waiting for transfers between devices: 79.1 us -> none  [per_device(): first_all = lax.all_gather(first, 'tp', axis=0, tiled=True)]
  transfers between devices with their start and end apart: 34 -> 36, of which waited for: 26 -> 28; matrix products, arithmetic and copies ran while one was open for 27% -> 27% of each run, Pallas kernels for 0% -> 0%
where the time goes in v1:
time: 1700 us; the launch traced here: 1690 us
  waiting for transfers between devices  1090 us (64%)
  matrix products  335 us (20%)
  other arithmetic  122 us (7%)
  blocking collectives  80.3 us (5%)
  local copies, waits for them, and re-layouts  21.7 us (1%)
  starting transfers between devices  20.3 us (1%)
  between operations  17.7 us (1%)
    reduce_scatter x2, waiting for transfers between devices, per_device(): lax.psum_scatter(key_buffer.astype(jnp.bfloat16), 'ctx', scatter_dimensio...  222 us
    reduce_scatter x2, waiting for transfers between devices, per_device(): lax.psum_scatter(project_rows(hidden_b, down_full).astype(jnp.bfloat16),...  86 us
    all_gather x2, waiting for transfers between devices, per_device(): upstream_all = lax.all_gather(upstream_b, 'tp', axis=0, tiled=True)  83.6 us
    ppermute x4, waiting for transfers between devices, collected_by_bits(): lax.ppermute(blocks, axis, [(i, i ^ bit) for i in range(size)])  83.2 us
    all_gather x2, waiting for transfers between devices, per_device(): second_all = lax.all_gather(second, 'tp', axis=0, tiled=True)  80.8 us
    dot_general x14, matrix products, dot_last(): lax.dot_general(left, right, (((1,), (1,)), ((), ())), preferred_element_...  64.4 us
    reduce_scatter x1, waiting for transfers between devices, per_device(): lax.psum_scatter(up_acc, ('shard', 'ctx'), scatter_dimension=0, tiled=True)  58.2 us
    reduce_scatter x1, waiting for transfers between devices, per_device(): lax.psum_scatter(down_acc, ('shard', 'ctx'), scatter_dimension=1, tiled=T...  57.9 us
  transfers between devices with their start and end apart: 36, of which 28 were waited for; matrix products, arithmetic and copies ran while one was open for 27% of the time, Pallas kernels for 0%

profile of v1, /device:TPU:0, one launch (start us, length us, event | category | flops | bytes accessed | tf_op | source)
XLA Modules:
  0.0 1686.3 jit_solution(11471679756842796130)
XLA Ops:
  17.2 10.4 collective-permute-done
  33.1 13.9 collective-permute-done.2
  49.6 9.6 all_gather.34
  59.3 42.0 %collective-permute-done.1 = bf16[2,256,1024]{2,1,0:T(8,128)(2,1)} collective-permute-done((bf16[2,256,1024]{2,1,0:T(8,128)(2,1)}, bf16[2,256,1024]{2,1,0:T(8,128)(2,1)}, u32[]{:S(2)}, u32[]{:S(2)}) %collective-permute-start.1) | collective-permute-done | bytes 1048608 | tf_op jit(solution)/shard_map/ppermute | solution.py:23
  104.3 16.8 collective-permute-done.3
  126.1 9.2 all_gather.37
  141.9 9.8 all_gather.36
  152.7 11.8 all_gather.39
  171.9 10.8 reduce-scatter.20.cloned.1.call-start
  186.0 84.7 %conditional.2 = (f32[2,2,1024]{2,1,0:T(2,128)}, f32[2,2,1024]{2,1,0:T(2,128)}, f32[2,2,1024,64]{2,3,1,0:T(8,128)S(1)}, f32[2,2,1024]{2,1,0:T(2,128)S(1)}) conditional(s32[]{:T(128)} %convert_element_type.314, () %tuple.36, (s32[1024]{0:T(1024)S(1)}, bf16[4096,2,64]{0,2,1:T(8,128)(2,1)}, bf16[1024,2,2,64]{0,3,2,1:T(8,128)(2,1)}, ...), branch_computations={%region_3.4_spmd, %region_4.7_spmd} | conditional | flops 4517261312 | bytes 221909024 | solution.py:123
  191.8 27.3 %fusion.4 = (f32[2,2,1024]{2,1,0:T(2,128)S(1)}, f32[2,4096,1024,2]{2,1,3,0:T(8,128)}) fusion(pred[1024,4096]{0,1:T(8,128)(4,1)} %iota_compare_fusion, bf16[1024,2,2,64]{0,3,2,1:T(8,128)(2,1)} %get-tuple-element.116, bf16[4096,2,64]{0,2,1:T(8,128)(2,1)} %get-tuple-element.115), kind=kOutput, calls=%fused_computation.4 | convolution fusion | flops 2197811200 | bytes 72892416 | tf_op jit(solution)/shard_map/cond/branch_1_fun/qkgd,nkd->kgqn/dot_general | solution.py:106
  219.7 23.8 %fusion.6 = f32[2,2,1024]{2,1,0:T(2,128)} fusion(f32[2,4096,1024,2]{2,1,3,0:T(8,128)} %get-tuple-element.326, f32[2,2,1024]{2,1,0:T(2,128)} %broadcast_maximum_fusion, pred[1024,4096]{0,1:T(8,128)(4,1)} %iota_compare_fusion), kind=kLoop, calls=%fused_computation.6 | loop fusion | flops 83881984 | bytes 71335936 | tf_op jit(solution)/shard_map/cond/branch_1_fun/reduce_sum | solution.py:114
  243.5 26.4 %fusion.7 = f32[2,2,1024,64]{2,3,1,0:T(8,128)S(1)} fusion(f32[2,4096,1024,2]{2,1,3,0:T(8,128)} %get-tuple-element.326, f32[2,2,1024]{2,1,0:T(2,128)} %broadcast_maximum_fusion, pred[1024,4096]{0,1:T(8,128)(4,1)} %iota_compare_fusion, bf16[4096,2,64]{0,2,1:T(8,128)(2,1)} %get-tuple-element.117), kind=kOutput, calls=%fused_computation.7 | convolution fusion | flops 2231369728 | bytes 73416704 | tf_op jit(solution)/shard_map/cond/branch_1_fun/kgqn,nkd->kgqd/dot_general | solution.py:115
  276.8 83.5 %conditional.3 = (f32[2,2,1024]{2,1,0:T(2,128)}, f32[2,2,1024]{2,1,0:T(2,128)}, f32[2,2,1024,64]{2,3,1,0:T(8,128)S(1)}, f32[2,2,1024]{2,1,0:T(2,128)S(1)}) conditional(s32[]{:T(128)} %convert_element_type.314, () %tuple.38, (s32[1024]{0:T(1024)S(1)}, bf16[4096,2,64]{0,2,1:T(8,128)(2,1)}, bf16[1024,2,2,64]{0,3,2,1:T(8,128)(2,1)}, ...), branch_computations={%region_13.14_spmd, %region_14.17_spmd} | conditional | flops 4517261312 | bytes 230297696 | solution.py:123
  282.6 26.1 %fusion.16 = (f32[2,2,1024]{2,1,0:T(2,128)S(1)}, f32[2,4096,1024,2]{2,1,3,0:T(8,128)}) fusion(pred[1024,4096]{0,1:T(8,128)(4,1)} %iota_compare_fusion.1, bf16[1024,2,2,64]{0,3,2,1:T(8,128)(2,1)} %get-tuple-element.120, bf16[4096,2,64]{0,2,1:T(8,128)(2,1)S(1)} %copy-done.25), kind=kOutput, calls=%fused_computation.19 | convolution fusion | flops 2197811200 | bytes 72892416 | tf_op jit(solution)/shard_map/cond/branch_1_fun/qkgd,nkd->kgqn/dot_general | solution.py:106
  309.3 24.1 %fusion.18 = f32[2,2,1024]{2,1,0:T(2,128)} fusion(f32[2,4096,1024,2]{2,1,3,0:T(8,128)} %get-tuple-element.328, f32[2,2,1024]{2,1,0:T(2,128)} %broadcast_maximum_fusion.1, pred[1024,4096]{0,1:T(8,128)(4,1)} %iota_compare_fusion.1), kind=kLoop, calls=%fused_computation.21 | loop fusion | flops 83881984 | bytes 71335936 | tf_op jit(solution)/shard_map/cond/branch_1_fun/reduce_sum | solution.py:114
  333.4 26.1 %fusion.19 = f32[2,2,1024,64]{2,3,1,0:T(8,128)S(1)} fusion(f32[2,4096,1024,2]{2,1,3,0:T(8,128)} %get-tuple-element.328, f32[2,2,1024]{2,1,0:T(2,128)} %broadcast_maximum_fusion.1, pred[1024,4096]{0,1:T(8,128)(4,1)} %iota_compare_fusion.1, bf16[4096,2,64]{0,2,1:T(8,128)(2,1)S(1)} %copy-done.115), kind=kOutput, calls=%fused_computation.22 | convolution fusion | flops 2231369728 | bytes 73416704 | tf_op jit(solution)/shard_map/cond/branch_1_fun/kgqn,nkd->kgqd/dot_general | solution.py:115
  364.7 43.4 %reduce-scatter.24.cloned.1.call-done = bf16[256,1024]{1,0:T(8,128)(2,1)} async-done(((bf16[1024,1024]{1,0:T(8,128)(2,1)}), bf16[256,1024]{1,0:T(8,128)(2,1)}) %reduce-scatter.24.cloned.1.call-update) | async-done | bytes 524304 | tf_op jit(solution)/shard_map/reduce_scatter | solution.py:249
  416.6 40.9 %all-gather.20.cloned.1.call-done = bf16[1024,1024]{1,0:T(8,128)(2,1)} async-done(((bf16[256,1024]{1,0:T(8,128)(2,1)}), bf16[1024,1024]{1,0:T(8,128)(2,1)}) %all-gather.20.cloned.1.call-update) | async-done | bytes 2097168 | tf_op jit(solution)/shard_map/all_gather | solution.py:257
  464.9 22.1 %all-gather.24.cloned.1.call-done = bf16[1024,1152]{1,0:T(8,128)(2,1)} async-done(((bf16[128,1152]{1,0:T(8,128)(2,1)}), bf16[1024,1152]{1,0:T(8,128)(2,1)}) %all-gather.24.cloned.1.call-update) | async-done | bytes 2359312 | tf_op jit(solution)/shard_map/all_gather | solution.py:85
  494.4 39.8 %all-gather.38.cloned.1.call-done = bf16[1,1024,1024]{2,1,0:T(8,128)(2,1)} async-done(((bf16[1,256,1024]{2,1,0:T(8,128)(2,1)}), bf16[1,1024,1024]{2,1,0:T(8,128)(2,1)}) %all-gather.38.cloned.1.call-update) | async-done | bytes 2097168 | tf_op jit(solution)/shard_map/all_gather | solution.py:281
  534.1 29.9 %all-gather.26.cloned.1.call-done = bf16[1152,1024]{1,0:T(8,128)(2,1)} async-done(((bf16[1152,128]{1,0:T(8,128)(2,1)}), bf16[1152,1024]{1,0:T(8,128)(2,1)}) %all-gather.26.cloned.1.call-update) | async-done | bytes 2359312 | tf_op jit(solution)/shard_map/all_gather | solution.py:86
  564.0 10.8 multiply_convert_fusion.2
  582.9 39.9 %all-gather.32.cloned.1.call-done = bf16[1024,1024]{1,0:T(8,128)(2,1)} async-done(((bf16[256,1024]{1,0:T(8,128)(2,1)}), bf16[1024,1024]{1,0:T(8,128)(2,1)}) %all-gather.32.cloned.1.call-update) | async-done | bytes 2097168 | tf_op jit(solution)/shard_map/all_gather | solution.py:257
  634.9 43.8 %all-gather.40.cloned.1.call-done = bf16[1,1024,1024]{2,1,0:T(8,128)(2,1)} async-done(((bf16[1,256,1024]{2,1,0:T(8,128)(2,1)}), bf16[1,1024,1024]{2,1,0:T(8,128)(2,1)}) %all-gather.40.cloned.1.call-update) | async-done | bytes 2097168 | tf_op jit(solution)/shard_map/all_gather | solution.py:281
  678.7 10.9 multiply_convert_fusion
  704.2 35.9 %reduce-scatter.36.cloned.1.call-done = bf16[256,1024]{1,0:T(8,128)(2,1)} async-done(((bf16[1024,1024]{1,0:T(8,128)(2,1)}), bf16[256,1024]{1,0:T(8,128)(2,1)}) %reduce-scatter.36.cloned.1.call-update) | async-done | bytes 524304 | tf_op jit(solution)/shard_map/reduce_scatter | solution.py:290
  742.9 42.7 %reduce-scatter.26.cloned.1.call-done = bf16[256,1024]{1,0:T(8,128)(2,1)} async-done(((bf16[1024,1024]{1,0:T(8,128)(2,1)}), bf16[256,1024]{1,0:T(8,128)(2,1)}) %reduce-scatter.26.cloned.1.call-update) | async-done | bytes 524304 | tf_op jit(solution)/shard_map/reduce_scatter | solution.py:263
  790.9 43.4 %all-gather.34.cloned.1.call-done = bf16[1024,1024]{1,0:T(8,128)(2,1)} async-done(((bf16[256,1024]{1,0:T(8,128)(2,1)}), bf16[1024,1024]{1,0:T(8,128)(2,1)}) %all-gather.34.cloned.1.call-update) | async-done | bytes 2097168 | tf_op jit(solution)/shard_map/all_gather | solution.py:300
  839.3 35.1 %while.30 = (s32[]{:T(128)}, f32[1024,2,2,64]{0,3,2,1:T(8,128)S(1)}, bf16[4096,2,64]{0,2,1:T(8,128)(2,1)}, bf16[4096,2,64]{0,2,1:T(8,128)(2,1)}, s32[]{:T(128)},...) while((s32[]{:T(128)}, ...), condition=%wide.region_23.24_spmd.clone, body=%wide.region_22.23_spmd.clone.sunk | while | flops 2728003584 | bytes 93126936 | solution.py:173
  839.3 9.3 fusion.339
  849.3 9.2 fusion.340
  886.0 37.1 %while.31 = (s32[]{:T(128)}, f32[1024,2,2,64]{0,3,2,1:T(8,128)S(1)}, bf16[4096,2,64]{0,2,1:T(8,128)(2,1)}, bf16[4096,2,64]{0,2,1:T(8,128)(2,1)}, s32[]{:T(128)},...) while((s32[]{:T(128)}, ...), condition=%wide.region_33.34_spmd.clone, body=%wide.region_32.33_spmd.clone.sunk | while | flops 2728003584 | bytes 95224120 | solution.py:173
  886.2 9.4 fusion.354
  913.0 10.1 fusion.358
  933.0 70.2 %reduce-scatter.30.cloned.1.call-done = bf16[1024,2,64]{0,2,1:T(8,128)(2,1)} async-done(((bf16[4096,2,64]{0,2,1:T(8,128)(2,1)}), bf16[1024,2,64]{0,2,1:T(8,128)(2,1)}) %reduce-scatter.30.cloned.1.call-update) | async-done | bytes 262160 | tf_op jit(solution)/shard_map/reduce_scatter | solution.py:315
  1005.0 152.0 %reduce-scatter.38.cloned.1.call-done = bf16[1024,2,64]{0,2,1:T(8,128)(2,1)} async-done(((bf16[4096,2,64]{0,2,1:T(8,128)(2,1)}), bf16[1024,2,64]{0,2,1:T(8,128)(2,1)}) %reduce-scatter.38.cloned.1.call-update) | async-done | bytes 262160 | tf_op jit(solution)/shard_map/reduce_scatter | solution.py:315
  1164.1 20.4 %reduce-scatter.32.cloned.1.call-done = bf16[1024,2,64]{0,2,1:T(8,128)(2,1)} async-done(((bf16[4096,2,64]{0,2,1:T(8,128)(2,1)}), bf16[1024,2,64]{0,2,1:T(8,128)(2,1)}) %reduce-scatter.32.cloned.1.call-update) | async-done | bytes 262160 | tf_op jit(solution)/shard_map/reduce_scatter | solution.py:318
  1195.8 16.2 reduce-scatter.40.cloned.1.call-done
  1271.7 31.8 %reduce-scatter.42.cloned.1.call-done = bf16[256,1024]{1,0:T(8,128)(2,1)} async-done(((bf16[1024,1024]{1,0:T(8,128)(2,1)}), bf16[256,1024]{1,0:T(8,128)(2,1)}) %reduce-scatter.42.cloned.1.call-update) | async-done | bytes 524304 | tf_op jit(solution)/shard_map/reduce_scatter | solution.py:334
  1305.6 43.3 %reduce-scatter.22.cloned.1.call-done = bf16[256,1024]{1,0:T(8,128)(2,1)} async-done(((bf16[1024,1024]{1,0:T(8,128)(2,1)}), bf16[256,1024]{1,0:T(8,128)(2,1)}) %reduce-scatter.22.cloned.1.call-update) | async-done | bytes 524304 | tf_op jit(solution)/shard_map/reduce_scatter | solution.py:263
  1352.2 39.9 %all-reduce.8 = (f32[1024]{0:T(1024)}, f32[1024]{0:T(1024)}, f32[64]{0:T(128)}, f32[64]{0:T(128)}) all-reduce(f32[1024]{0:T(1024)S(1)} %add.363, f32[1024]{0:T(1024)S(1)} %add.364, f32[64]{0:T(128)S(1)} %add.365, f32[64]{0:T(128)S(1)} %add.366), channel_id=1, replica_groups=mesh['shard'=2,'ctx'=4,'tp'=4] {'shard','ctx','tp'}, use_global_device_ids=true, to_apply=%region_49.50 | all-reduce | flops 2176 | bytes 17408 | tf_op jit(solution)/shard_map/psum | solution.py:355
  1406.7 58.2 %reduce-scatter.54.cloned.1.call-done = f32[128,1152]{1,0:T(8,128)} async-done(((f32[1024,1152]{1,0:T(8,128)}), f32[128,1152]{1,0:T(8,128)}) %reduce-scatter.54.cloned.1.call-update) | async-done | bytes 589840 | tf_op jit(solution)/shard_map/reduce_scatter | solution.py:352
  1464.8 57.9 %reduce-scatter.56.cloned.1.call-done = f32[1152,128]{1,0:T(8,128)} async-done(((f32[1152,1024]{1,0:T(8,128)}), f32[1152,128]{1,0:T(8,128)}) %reduce-scatter.56.cloned.1.call-update) | async-done | bytes 589840 | tf_op jit(solution)/shard_map/reduce_scatter | solution.py:353
  1522.8 40.0 %reduce-scatter.44.cloned.1.call-done = f32[128,256]{1,0:T(8,128)} async-done(((f32[1024,256]{1,0:T(8,128)}), f32[128,256]{1,0:T(8,128)}) %reduce-scatter.44.cloned.1.call-update) | async-done | bytes 131088 | tf_op jit(solution)/shard_map/reduce_scatter | solution.py:347
  1562.8 40.1 %reduce-scatter.50.cloned.1.call-done = f32[256,128]{1,0:T(8,128)} async-done(((f32[256,1024]{1,0:T(8,128)}), f32[256,128]{1,0:T(8,128)}) %reduce-scatter.50.cloned.1.call-update) | async-done | bytes 131088 | tf_op jit(solution)/shard_map/reduce_scatter | solution.py:350
  1602.9 38.1 %reduce-scatter.46.cloned.1.call-done = f32[128,128]{1,0:T(8,128)} async-done(((f32[1024,128]{1,0:T(8,128)}), f32[128,128]{1,0:T(8,128)}) %reduce-scatter.46.cloned.1.call-update) | async-done | bytes 65552 | tf_op jit(solution)/shard_map/reduce_scatter | solution.py:348
  1641.0 37.7 %reduce-scatter.48.cloned.1.call-done = f32[128,128]{1,0:T(8,128)} async-done(((f32[1024,128]{1,0:T(8,128)}), f32[128,128]{1,0:T(8,128)}) %reduce-scatter.48.cloned.1.call-update) | async-done | bytes 65552 | tf_op jit(solution)/shard_map/reduce_scatter | solution.py:349
  (461 shorter events, 292.8 us)
Async XLA Ops:
  8.0 178.0 %all-gather.16.cloned.1.call-start = ((), (), s32[]{:S(2)}) async-start(), calls=%async_computation.19 | async-start | bytes 1310720 | tf_op jit(solution)/shard_map/all_gather | solution.py:100
  11.7 15.8 collective-permute-start
  14.8 32.3 %collective-permute-start.2 = (bf16[1,256,1024]{2,1,0:T(8,128)(2,1)S(1)}, bf16[1,256,1024]{2,1,0:T(8,128)(2,1)}, u32[]{:S(2)}, u32[]{:S(2)}) collective-permute-start(bf16[1,256,1024]{2,1,0:T(8,128)(2,1)S(1)} %get-tuple-element.349), channel_id=1, source_target_pairs={{0,1},{1,0},{2,3},{3,2},{4,5},{5,4},{6,7},{7,6},{8,9},{9,8},{10,11... | collective-permute-start | bytes 1572872 | tf_op jit(solution)/shard_map/ppermute | solution.py:23
  29.0 72.4 %collective-permute-start.1 = (bf16[2,256,1024]{2,1,0:T(8,128)(2,1)}, bf16[2,256,1024]{2,1,0:T(8,128)(2,1)}, u32[]{:S(2)}, u32[]{:S(2)}) collective-permute-start(bf16[2,256,1024]{2,1,0:T(8,128)(2,1)} %get-tuple-element.359), channel_id=1, source_target_pairs={{0,2},{1,3},{2,0},{3,1},{4,6},{5,7},{6,4},{7,5},{8,10},{9,11},{10,... | collective-permute-start | bytes 3145736 | tf_op jit(solution)/shard_map/ppermute | solution.py:23
  33.1 151.8 %copy-start.12 = (f32[1024,64]{0,1:T(8,128)}, f32[1024,64]{0,1:T(8,128)S(1)}, u32[]{:S(2)}) copy-start(f32[1024,64]{0,1:T(8,128)S(1)} %pad_maximum_fusion.6) | copy-start | bytes 786436
  49.6 71.6 %collective-permute-start.3 = (bf16[2,256,1024]{2,1,0:T(8,128)(2,1)}, bf16[2,256,1024]{2,1,0:T(8,128)(2,1)}, u32[]{:S(2)}, u32[]{:S(2)}) collective-permute-start(bf16[2,256,1024]{2,1,0:T(8,128)(2,1)} %get-tuple-element.363), channel_id=1, source_target_pairs={{0,2},{1,3},{2,0},{3,1},{4,6},{5,7},{6,4},{7,5},{8,10},{9,11},{10,... | collective-permute-start | bytes 3145736 | tf_op jit(solution)/shard_map/ppermute | solution.py:23
  126.1 59.9 %all-gather.18.cloned.1.call-start = ((), (), s32[]{:S(2)}) async-start(), calls=%async_computation.20 | async-start | bytes 1310720 | tf_op jit(solution)/shard_map/all_gather | solution.py:101
  138.6 138.2 %all-gather.28.cloned.1.call-start = ((), (), s32[]{:S(2)}) async-start(), calls=%async_computation.27 | async-start | bytes 1310720 | tf_op jit(solution)/shard_map/all_gather | solution.py:100
  138.7 137.0 %copy-start.14 = (f32[1024,64]{0,1:T(8,128)}, f32[1024,64]{0,1:T(8,128)S(1)}, u32[]{:S(2)}) copy-start(f32[1024,64]{0,1:T(8,128)S(1)} %pad_maximum_fusion.8) | copy-start | bytes 786436
  141.8 135.0 %all-gather.30.cloned.1.call-start = ((), (), s32[]{:S(2)}) async-start(), calls=%async_computation.28 | async-start | bytes 1310720 | tf_op jit(solution)/shard_map/all_gather | solution.py:101
  171.9 192.8 %reduce-scatter.20.cloned.1.call-start = ((), (), s32[]{:S(2)}) async-start(), calls=%async_computation.21 | async-start | bytes 2621440 | tf_op jit(solution)/shard_map/reduce_scatter | solution.py:249
  275.1 133.1 %reduce-scatter.24.cloned.1.call-start = ((), (), s32[]{:S(2)}) async-start(), calls=%async_computation.29 | async-start | bytes 2621440 | tf_op jit(solution)/shard_map/reduce_scatter | solution.py:249
  364.1 52.6 %all-gather.22.cloned.1.call-start = ((), (), s32[]{:S(2)}) async-start(), calls=%async_computation.23 | async-start | bytes 2654208 | tf_op jit(solution)/shard_map/all_gather | solution.py:84
  364.7 92.9 %all-gather.20.cloned.1.call-start = ((), (), s32[]{:S(2)}) async-start(), calls=%async_computation.22 | async-start | bytes 2621440 | tf_op jit(solution)/shard_map/all_gather | solution.py:257
  409.8 375.8 %copy-start.88 = (f32[256]{0:T(256)}, f32[256]{0:T(256)S(1)}, u32[]{:S(2)}) copy-start(f32[256]{0:T(256)S(1)} %fusion.177) | copy-start | bytes 3076
  409.8 375.8 %copy-start.86 = (f32[256]{0:T(256)}, f32[256]{0:T(256)S(1)}, u32[]{:S(2)}) copy-start(f32[256]{0:T(256)S(1)} %fusion.179) | copy-start | bytes 3076
  412.5 74.4 %all-gather.24.cloned.1.call-start = ((), (), s32[]{:S(2)}) async-start(), calls=%async_computation.24 | async-start | bytes 2654208 | tf_op jit(solution)/shard_map/all_gather | solution.py:85
  413.1 121.0 %all-gather.38.cloned.1.call-start = ((), (), s32[]{:S(2)}) async-start(), calls=%async_computation.49 | async-start | bytes 2621440 | tf_op jit(solution)/shard_map/all_gather | solution.py:281
  414.3 149.7 %all-gather.26.cloned.1.call-start = ((), (), s32[]{:S(2)}) async-start(), calls=%async_computation.25 | async-start | bytes 2654208 | tf_op jit(solution)/shard_map/all_gather | solution.py:86
  415.1 207.8 %all-gather.32.cloned.1.call-start = ((), (), s32[]{:S(2)}) async-start(), calls=%async_computation.30 | async-start | bytes 2621440 | tf_op jit(solution)/shard_map/all_gather | solution.py:257
  415.8 262.9 %all-gather.40.cloned.1.call-start = ((), (), s32[]{:S(2)}) async-start(), calls=%async_computation.50 | async-start | bytes 2621440 | tf_op jit(solution)/shard_map/all_gather | solution.py:281
  416.4 287.9 %reduce-scatter.28.cloned.1.call-start = ((), (), s32[]{:S(2)}) async-start(), calls=%async_computation.32 | async-start | bytes 2621440 | tf_op jit(solution)/shard_map/reduce_scatter | solution.py:290
  582.5 157.7 %reduce-scatter.36.cloned.1.call-start = ((), (), s32[]{:S(2)}) async-start(), calls=%async_computation.37 | async-start | bytes 2621440 | tf_op jit(solution)/shard_map/reduce_scatter | solution.py:290
  697.3 88.4 %reduce-scatter.26.cloned.1.call-start = ((), (), s32[]{:S(2)}) async-start(), calls=%async_computation.31 | async-start | bytes 2621440 | tf_op jit(solution)/shard_map/reduce_scatter | solution.py:263
  704.0 130.3 %all-gather.34.cloned.1.call-start = ((), (), s32[]{:S(2)}) async-start(), calls=%async_computation.33 | async-start | bytes 2621440 | tf_op jit(solution)/shard_map/all_gather | solution.py:300
  789.3 90.8 %all-gather.36.cloned.1.call-start = ((), (), s32[]{:S(2)}) async-start(), calls=%async_computation.38 | async-start | bytes 2621440 | tf_op jit(solution)/shard_map/all_gather | solution.py:300
  790.8 212.3 %reduce-scatter.30.cloned.1.call-start = ((), (), s32[]{:S(2)}) async-start(), calls=%async_computation.34 | async-start | bytes 1310720 | tf_op jit(solution)/shard_map/reduce_scatter | solution.py:315
  874.5 282.6 %reduce-scatter.38.cloned.1.call-start = ((), (), s32[]{:S(2)}) async-start(), calls=%async_computation.39 | async-start | bytes 1310720 | tf_op jit(solution)/shard_map/reduce_scatter | solution.py:315
  923.1 261.4 %reduce-scatter.32.cloned.1.call-start = ((), (), s32[]{:S(2)}) async-start(), calls=%async_computation.35 | async-start | bytes 1310720 | tf_op jit(solution)/shard_map/reduce_scatter | solution.py:318
  924.7 287.2 %reduce-scatter.40.cloned.1.call-start = ((), (), s32[]{:S(2)}) async-start(), calls=%async_computation.40 | async-start | bytes 1310720 | tf_op jit(solution)/shard_map/reduce_scatter | solution.py:318
  930.1 229.1 %copy-start.35 = (f32[1024,2,64]{0,2,1:T(8,128)S(1)}, f32[1024,2,64]{0,2,1:T(8,128)}, u32[]{:S(2)}) copy-start(f32[1024,2,64]{0,2,1:T(8,128)} %copy-done.34) | copy-start | bytes 1572868
  930.1 229.1 %copy-start.37 = (f32[1024,2,64]{0,2,1:T(8,128)S(1)}, f32[1024,2,64]{0,2,1:T(8,128)}, u32[]{:S(2)}) copy-start(f32[1024,2,64]{0,2,1:T(8,128)} %copy-done.36) | copy-start | bytes 1572868
  930.1 229.2 %copy-start.64 = (f32[1024,2]{0,1:T(2,128)S(1)}, f32[1024,2]{0,1:T(2,128)}, u32[]{:S(2)}) copy-start(f32[1024,2]{0,1:T(2,128)} %copy-done.63) | copy-start | bytes 24580
  930.1 229.2 %copy-start.66 = (f32[1024,2]{0,1:T(2,128)S(1)}, f32[1024,2]{0,1:T(2,128)}, u32[]{:S(2)}) copy-start(f32[1024,2]{0,1:T(2,128)} %copy-done.65) | copy-start | bytes 24580
  930.1 229.2 %copy-start.103 = (f32[64]{0:T(128)S(1)}, f32[64]{0:T(128)}, u32[]{:S(2)}) copy-start(f32[64]{0:T(128)} %param.29) | copy-start | bytes 772
  932.9 227.9 %copy-start.79 = (f32[1024,2]{0,1:T(2,128)S(1)}, f32[1024,2]{0,1:T(2,128)}, u32[]{:S(2)}) copy-start(f32[1024,2]{0,1:T(2,128)} %copy-done.78) | copy-start | bytes 24580
  932.9 227.9 %copy-start.81 = (f32[1024,2]{0,1:T(2,128)S(1)}, f32[1024,2]{0,1:T(2,128)}, u32[]{:S(2)}) copy-start(f32[1024,2]{0,1:T(2,128)} %copy-done.80) | copy-start | bytes 24580
  932.9 338.8 %reduce-scatter.34.cloned.1.call-start = ((), (), s32[]{:S(2)}) async-start(), calls=%async_computation.36 | async-start | bytes 2621440 | tf_op jit(solution)/shard_map/reduce_scatter | solution.py:334
  1003.2 156.1 %copy-start.53 = (bf16[1024,2,64]{0,2,1:T(8,128)(2,1)S(1)}, bf16[1024,2,64]{0,2,1:T(8,128)(2,1)}, u32[]{:S(2)}) copy-start(bf16[1024,2,64]{0,2,1:T(8,128)(2,1)} %reduce-scatter.30.cloned.1.call-done) | copy-start | bytes 786436
  1190.2 113.3 %reduce-scatter.42.cloned.1.call-start = ((), (), s32[]{:S(2)}) async-start(), calls=%async_computation.41 | async-start | bytes 2621440 | tf_op jit(solution)/shard_map/reduce_scatter | solution.py:334
  1217.5 131.4 %reduce-scatter.22.cloned.1.call-start = ((), (), s32[]{:S(2)}) async-start(), calls=%async_computation.26 | async-start | bytes 2621440 | tf_op jit(solution)/shard_map/reduce_scatter | solution.py:263
  1224.3 182.4 %reduce-scatter.52.cloned.1.call-start = ((), (), s32[]{:S(2)}) async-start(), calls=%async_computation.46 | async-start | bytes 5308416 | tf_op jit(solution)/shard_map/reduce_scatter | solution.py:351
  1234.2 230.7 %reduce-scatter.54.cloned.1.call-start = ((), (), s32[]{:S(2)}) async-start(), calls=%async_computation.47 | async-start | bytes 5308416 | tf_op jit(solution)/shard_map/reduce_scatter | solution.py:352
  1243.9 278.9 %reduce-scatter.56.cloned.1.call-start = ((), (), s32[]{:S(2)}) async-start(), calls=%async_computation.48 | async-start | bytes 5308416 | tf_op jit(solution)/shard_map/reduce_scatter | solution.py:353
  1254.4 308.4 %reduce-scatter.44.cloned.1.call-start = ((), (), s32[]{:S(2)}) async-start(), calls=%async_computation.42 | async-start | bytes 1179648 | tf_op jit(solution)/shard_map/reduce_scatter | solution.py:347
  1260.5 342.4 %reduce-scatter.50.cloned.1.call-start = ((), (), s32[]{:S(2)}) async-start(), calls=%async_computation.45 | async-start | bytes 1179648 | tf_op jit(solution)/shard_map/reduce_scatter | solution.py:350
  1264.8 376.2 %reduce-scatter.46.cloned.1.call-start = ((), (), s32[]{:S(2)}) async-start(), calls=%async_computation.43 | async-start | bytes 589824 | tf_op jit(solution)/shard_map/reduce_scatter | solution.py:348
  1268.3 410.4 %reduce-scatter.48.cloned.1.call-start = ((), (), s32[]{:S(2)}) async-start(), calls=%async_computation.44 | async-start | bytes 589824 | tf_op jit(solution)/shard_map/reduce_scatter | solution.py:349
  (111 other events, 2084.4 us)
Sparse Core Ops, SparseCore 0:
  126.2 17.8 all-gather.15
  146.2 18.8 all-gather.17
  166.6 16.7 all-gather.27
  184.8 16.7 all-gather.29
  275.2 43.8 reduce-scatter.19
  364.2 43.9 reduce-scatter.23
  582.6 62.7 reduce-scatter.27
  697.4 42.7 reduce-scatter.35
  742.4 43.1 reduce-scatter.25
  874.6 128.5 reduce-scatter.29
  1005.7 151.2 reduce-scatter.37
  1159.6 24.8 reduce-scatter.31
  1187.0 24.8 reduce-scatter.39
  1214.2 43.8 reduce-scatter.33
  1260.2 43.1 reduce-scatter.41
  1305.7 43.1 reduce-scatter.21
  1352.8 53.8 reduce-scatter.51
  1410.9 53.8 reduce-scatter.53
  1468.9 53.8 reduce-scatter.55
  1526.7 36.0 reduce-scatter.43
  1566.9 35.9 reduce-scatter.49
  1606.8 34.0 reduce-scatter.45
  1644.6 34.0 reduce-scatter.47
Sparse Core Ops, SparseCore 1:
  366.4 28.9 all-gather.21
  412.6 44.9 all-gather.19
  459.3 27.6 all-gather.23
  488.5 45.5 all-gather.37
  536.0 28.0 all-gather.25
  565.7 57.1 all-gather.31
  624.4 54.3 all-gather.39
  789.4 44.9 all-gather.33
  835.7 44.3 all-gather.35
